TPU v7x, 32 devices: a whole 2x2x4 slice. The times are simulated.
32 devices in a mesh: dp: 4 (over z), ctx: 4 (over x, core), tensor: 2 (over y).
Axes of the slice: x: 2, y: 2, z: 4, core: 2. Of those that a mesh axis runs over, the one named last changes fastest.
Arguments:
- layer_input: bfloat16 [4, 1024, 2048], P('dp', 'ctx'), may hold values from -6 to 6
- output_grad: bfloat16 [4, 1024, 2048], P('dp', 'ctx'), may hold values from -6 to 6
- prefix: int32 [4], P('dp'), may hold values from 204 to 1024
- attn_gain: float32 [2048], replicated, may hold values from 0.1 to 1.9
- w_query: bfloat16 [2048, 2048], P(None, 'tensor'), may hold values from -0.125 to 0.125
- w_key: bfloat16 [2048, 512], P(None, 'tensor'), may hold values from -0.125 to 0.125
- w_value: bfloat16 [2048, 512], P(None, 'tensor'), may hold values from -0.125 to 0.125
- w_out: bfloat16 [2048, 2048], P('tensor'), may hold values from -1 to 1
- mlp_gain: float32 [2048], replicated, may hold values from 0.1 to 1.9
- w_gate: bfloat16 [2048, 8192], P(None, 'tensor'), may hold values from -0.125 to 0.125
- w_up: bfloat16 [2048, 8192], P(None, 'tensor'), may hold values from -0.125 to 0.125
- w_down: bfloat16 [8192, 2048], P('tensor'), may hold values from -0.0625 to 0.0625
Outputs:
- layer_output: bfloat16 [4, 1024, 2048], P('dp', 'ctx')
- input_grad: float32 [4, 1024, 2048], P('dp', 'ctx')
- d_attn_gain: float32 [2048], P(('dp', 'ctx'))
- d_query: float32 [2048, 2048], P(('dp', 'ctx'), 'tensor')
- d_key: float32 [2048, 512], P(('dp', 'ctx'), 'tensor')
- d_value: float32 [2048, 512], P(('dp', 'ctx'), 'tensor')
- d_out_proj: float32 [2048, 2048], P('tensor', ('dp', 'ctx'))
- d_mlp_gain: float32 [2048], P(('dp', 'ctx'))
- d_gate: float32 [2048, 8192], P(('dp', 'ctx'), 'tensor')
- d_up: float32 [2048, 8192], P(('dp', 'ctx'), 'tensor')
- d_down: float32 [8192, 2048], P('tensor', ('dp', 'ctx'))
All inputs are finite; a program needn't handle non-finite values.
Results may differ from a plain program's by a relative error of at most 0.024.
Values may be sent and summed in bfloat16 or wider, within the bound.
A program may use at most 256 MiB of HBM per device.

v0:
```python
import jax
import jax.numpy as jnp
from jax import lax
from jax.sharding import PartitionSpec as P

HD = 64
EPS = 1e-05
ROPE_BASE = 500000.0
NEG = -1e30
BF = jnp.bfloat16
F32 = jnp.float32


def dot_plain(left, right):
    return jnp.dot(left, right, preferred_element_type=F32)


def dot_right(left, right):
    return lax.dot_general(left, right, (((1,), (1,)), ((), ())), preferred_element_type=F32)


def dot_left(left, right):
    return lax.dot_general(left, right, (((0,), (0,)), ((), ())), preferred_element_type=F32)


def normed(v, gain):
    return v * lax.rsqrt(jnp.mean(v * v, axis=-1, keepdims=True) + EPS) * gain


def norm_back(v, gain, grad):
    factor = lax.rsqrt(jnp.mean(v * v, axis=-1, keepdims=True) + EPS)
    unit = v * factor
    d_unit = grad * gain
    d_gain = jnp.sum(grad * unit, axis=0)
    d_v = factor * (d_unit - unit * jnp.mean(d_unit * unit, axis=-1, keepdims=True))
    return (d_v, d_gain)


def rotate(t, cosine, sine):
    half = t.shape[-1] // 2
    first, second = (t[..., :half], t[..., half:])
    return jnp.concatenate(
        [first * cosine - second * sine, second * cosine + first * sine], axis=-1
    )


def rotate_back(t, cosine, sine):
    half = t.shape[-1] // 2
    first, second = (t[..., :half], t[..., half:])
    return jnp.concatenate(
        [first * cosine + second * sine, second * cosine - first * sine], axis=-1
    )


def score_block(query5, key_all, allowed):
    scores = jnp.einsum("scngd,slnd->sngcl", query5, key_all, preferred_element_type=F32) * HD ** (
        -0.5
    )
    return jnp.where(allowed[:, None, None], scores, NEG)


def build(ndp, nctx, nten):

    def pull(v, axis, n, s):
        return lax.ppermute(v, axis, [((i + s) % n, i) for i in range(n)])

    def flip(v, axis, n, bit):
        return lax.ppermute(v, axis, [(i, i ^ bit) for i in range(n)])

    def tensor_sum(v):
        low = v.astype(BF)
        if nten == 2:
            return low.astype(F32) + flip(low, "tensor", 2, 1).astype(F32)
        return lax.psum(low, "tensor").astype(F32)

    def gather_dp(v):
        rows = v.shape[0] // nten
        part = lax.dynamic_slice_in_dim(v, lax.axis_index("tensor") * rows, rows, 0)
        pieces = [v]
        for s in range(1, ndp):
            got = pull(part, "dp", ndp, s)
            pieces.append(got)
            for t in range(1, nten):
                pieces.append(pull(got, "tensor", nten, t))
        return jnp.concatenate(pieces, axis=0)

    def ctx_sum(full):
        r = full.shape[0] // (ndp * nctx)
        me = lax.axis_index("ctx")
        work = full.reshape(ndp, nctx, r, full.shape[1])
        bit = 1
        while bit < nctx:
            left = work.shape[1] // 2
            work = work.reshape(ndp, left, 2, r, full.shape[1])
            mine = me // bit % 2
            keep = lax.dynamic_index_in_dim(work, mine, 2, keepdims=False)
            give = lax.dynamic_index_in_dim(work, 1 - mine, 2, keepdims=False)
            got = flip(give, "ctx", nctx, bit)
            work = (keep.astype(F32) + got.astype(F32)).astype(BF)
            bit *= 2
        return work.reshape(ndp, r, full.shape[1])

    def finish_slices(full):
        got = lax.all_to_all(ctx_sum(full), "dp", 0, 0, tiled=True)
        return jnp.swapaxes(got, 0, 1).reshape(got.shape[1], -1).astype(F32)

    def finish_sum(full):
        got = lax.all_to_all(ctx_sum(full), "dp", 0, 0, tiled=True)
        return jnp.sum(got.astype(F32), axis=0)

    def local(
        layer_input,
        output_grad,
        prefix,
        attn_gain,
        w_query,
        w_key,
        w_value,
        w_out,
        mlp_gain,
        w_gate,
        w_up,
        w_down,
    ):
        seqs, span, width = layer_input.shape
        q_heads = w_query.shape[1] // HD
        kv_heads = w_key.shape[1] // HD
        group = q_heads // kv_heads
        zi = lax.axis_index("dp")
        rows = layer_input.astype(F32).reshape(seqs * span, width)
        grad_low = output_grad.reshape(seqs * span, width)
        grad_rows = grad_low.astype(F32)
        grad_all = gather_dp(grad_low)
        first = lax.axis_index("ctx") * span
        position = (first + jnp.arange(span)).astype(F32)
        frequency = ROPE_BASE ** (-jnp.arange(HD // 2).astype(F32) * 2.0 / HD)
        angle = position[:, None] * frequency[None, :]
        cosine = jnp.cos(angle)[None, :, None, :]
        sine = jnp.sin(angle)[None, :, None, :]
        normed1 = normed(rows, attn_gain).astype(BF)
        query = rotate(
            dot_plain(normed1, w_query).reshape(seqs, span, q_heads, HD), cosine, sine
        ).astype(BF)
        keyed = rotate(
            dot_plain(normed1, w_key).reshape(seqs, span, kv_heads, HD), cosine, sine
        ).astype(BF)
        valued = dot_plain(normed1, w_value).astype(BF).reshape(seqs, span, kv_heads * HD)
        key_all, value_all = (
            lax.all_gather(keyed.reshape(seqs, span, kv_heads * HD), "ctx", axis=1, tiled=True),
            lax.all_gather(valued, "ctx", axis=1, tiled=True),
        )
        length = key_all.shape[1]
        key_all = key_all.reshape(seqs, length, kv_heads, HD)
        value_all = value_all.reshape(seqs, length, kv_heads, HD)
        query5 = query.reshape(seqs, span, kv_heads, group, HD)
        query_pos = first + jnp.arange(span)
        key_pos = jnp.arange(length)
        allowed = (key_pos[None, None, :] <= query_pos[None, :, None]) | (
            key_pos[None, None, :] < prefix[:, None, None]
        )
        scores = score_block(query5, key_all, allowed)
        top = jnp.max(scores, axis=-1, keepdims=True)
        exponent = jnp.exp(scores - top)
        total = jnp.sum(exponent, axis=-1, keepdims=True)
        log_total = top + jnp.log(total)
        probs_low = (exponent / total).astype(BF)
        attended = jnp.einsum("sngcl,slnd->scngd", probs_low, value_all, preferred_element_type=F32)
        attended = attended.astype(BF).reshape(seqs * span, q_heads * HD)
        resid = rows + tensor_sum(dot_plain(attended, w_out))
        normed2 = normed(resid, mlp_gain).astype(BF)
        normed2_all = gather_dp(normed2)
        gate = dot_plain(normed2, w_gate)
        up = dot_plain(normed2, w_up)
        act = (jax.nn.silu(gate) * up).astype(BF)

        def mlp_back(gate, up, d_act):
            sigmoid_gate = jax.nn.sigmoid(gate)
            d_gate_pre = (d_act * up * sigmoid_gate * (1.0 + gate * (1.0 - sigmoid_gate))).astype(
                BF
            )
            d_up_pre = (d_act * gate * sigmoid_gate).astype(BF)
            return (d_gate_pre, d_up_pre)

        d_act = dot_right(grad_low, w_down)
        d_gate_pre, d_up_pre = mlp_back(gate, up, d_act)
        back_terms = dot_right(d_gate_pre, w_gate) + dot_right(d_up_pre, w_up)
        d_normed2 = tensor_sum(back_terms)
        output = (resid + tensor_sum(dot_plain(act, w_down))).astype(BF)
        output = output.reshape(seqs, span, width)
        units = w_gate.shape[1] // ndp
        wg = lax.dynamic_slice_in_dim(w_gate, zi * units, units, 1)
        wu = lax.dynamic_slice_in_dim(w_up, zi * units, units, 1)
        wd = lax.dynamic_slice_in_dim(w_down, zi * units, units, 0)
        gate_s = dot_plain(normed2_all, wg)
        up_s = dot_plain(normed2_all, wu)
        d_act_s = dot_right(grad_all, wd)
        act_s = (jax.nn.silu(gate_s) * up_s).astype(BF)
        d_gate_s, d_up_s = mlp_back(gate_s, up_s, d_act_s)
        s_down = finish_slices(dot_left(grad_all, act_s).astype(BF)).T
        s_gate = finish_slices(dot_left(normed2_all, d_gate_s).astype(BF))
        s_up = finish_slices(dot_left(normed2_all, d_up_s).astype(BF))
        d_resid_norm, g_mlp_gain = norm_back(resid, mlp_gain, d_normed2)
        d_resid = grad_rows + d_resid_norm
        d_resid_low = d_resid.astype(BF)
        s_out = finish_sum(dot_left(d_resid_low, attended).astype(BF)).T
        d_attended = dot_right(d_resid_low, w_out).astype(BF).reshape(query5.shape)
        scores = score_block(query5, key_all, allowed)
        probs = jnp.exp(scores - log_total)
        probs_low = probs.astype(BF)
        d_probs = jnp.einsum("scngd,slnd->sngcl", d_attended, value_all, preferred_element_type=F32)
        delta = jnp.sum(probs * d_probs, axis=-1, keepdims=True)
        d_scores = (probs * (d_probs - delta)).astype(BF)
        scale = HD ** (-0.5)
        d_query = (
            jnp.einsum("sngcl,slnd->scngd", d_scores, key_all, preferred_element_type=F32) * scale
        )
        d_key_all = (
            jnp.einsum("sngcl,scngd->slnd", d_scores, query5, preferred_element_type=F32) * scale
        )
        d_value_all = jnp.einsum(
            "sngcl,scngd->slnd", probs_low, d_attended, preferred_element_type=F32
        )
        d_kv = jnp.concatenate(
            [
                d_key_all.reshape(length, kv_heads * HD).astype(BF),
                d_value_all.reshape(length, kv_heads * HD).astype(BF),
            ],
            axis=1,
        )
        d_kv = lax.psum_scatter(d_kv, "ctx", scatter_dimension=0, tiled=True).astype(F32)
        d_key, d_val = (d_kv[:, : kv_heads * HD], d_kv[:, kv_heads * HD :])
        d_qp = (
            rotate_back(d_query.reshape(seqs, span, q_heads, HD), cosine, sine)
            .astype(BF)
            .reshape(seqs * span, q_heads * HD)
        )
        d_kp = (
            rotate_back(d_key.reshape(seqs, span, kv_heads, HD), cosine, sine)
            .astype(BF)
            .reshape(seqs * span, kv_heads * HD)
        )
        d_vp = d_val.astype(BF).reshape(seqs * span, kv_heads * HD)
        front_terms = dot_right(d_qp, w_query) + dot_right(d_kp, w_key) + dot_right(d_vp, w_value)
        d_normed1 = tensor_sum(front_terms)
        d_rows_norm, g_attn_gain = norm_back(rows, attn_gain, d_normed1)
        d_input = d_resid + d_rows_norm
        d_input = d_input.reshape(seqs, span, width)
        s_qkv = finish_sum(
            dot_left(normed1, jnp.concatenate([d_qp, d_kp, d_vp], axis=1)).astype(BF)
        )
        nq, nk = (q_heads * HD, kv_heads * HD)
        s_query, s_key, s_value = (s_qkv[:, :nq], s_qkv[:, nq : nq + nk], s_qkv[:, nq + nk :])
        gains = jnp.stack([g_attn_gain, g_mlp_gain])
        gains = lax.psum_scatter(gains, ("dp", "ctx"), scatter_dimension=1, tiled=True)
        return (
            output,
            d_input,
            gains[0],
            s_query,
            s_key,
            s_value,
            s_out,
            gains[1],
            s_gate,
            s_up,
            s_down,
        )

    return local


def solution(mesh):
    sizes = mesh.shape
    return jax.shard_map(
        build(sizes["dp"], sizes["ctx"], sizes["tensor"]),
        mesh=mesh,
        in_specs=(
            P("dp", "ctx", None),
            P("dp", "ctx", None),
            P("dp"),
            P(),
            P(None, "tensor"),
            P(None, "tensor"),
            P(None, "tensor"),
            P("tensor", None),
            P(),
            P(None, "tensor"),
            P(None, "tensor"),
            P("tensor", None),
        ),
        out_specs=(
            P("dp", "ctx", None),
            P("dp", "ctx", None),
            P(("dp", "ctx")),
            P(("dp", "ctx"), "tensor"),
            P(("dp", "ctx"), "tensor"),
            P(("dp", "ctx"), "tensor"),
            P("tensor", ("dp", "ctx")),
            P(("dp", "ctx")),
            P(("dp", "ctx"), "tensor"),
            P(("dp", "ctx"), "tensor"),
            P("tensor", ("dp", "ctx")),
        ),
        check_vma=False,
    )
```

profile of v0, /device:TPU:0, one launch (start us, length us, event | category | flops | bytes accessed | tf_op | source)
XLA Modules:
  0.0 580.2 jit_solution(16229616995724655871)
XLA Ops:
  9.3 5.1 collective-permute-start.14
  18.7 7.6 %all-gather = bf16[1024,256]{1,0:T(8,128)(2,1)} all-gather(bf16[256,256]{1,0:T(8,128)(2,1)S(1)} %convolution_convert_fusion.8), channel_id=2, replica_groups=mesh['dp'=4,'ctx'=4,'tensor'=2] {'ctx'}, dimensions={0}, use_global_device_ids=true | all-gather | bytes 655360 | tf_op jit(solution)/shard_map/all_gather | solution.py:150
  31.8 7.8 %all_gather.7 = bf16[1,1024,256]{1,2,0:T(8,128)(2,1)S(1)} all-gather(bf16[1,256,256]{1,2,0:T(8,128)(2,1)S(1)} %bitcast.283), channel_id=1, replica_groups=mesh['dp'=4,'ctx'=4,'tensor'=2] {'ctx'}, dimensions={1}, use_global_device_ids=true | all-gather | bytes 655360 | tf_op jit(solution)/shard_map/all_gather | solution.py:149
  39.6 6.7 %copy.49 = bf16[2048,1024]{0,1:T(8,128)(2,1)} copy(bf16[2048,1024]{1,0:T(8,128)(2,1)} %param.16) | data formatting | bytes 8388608 | tf_op args[4]
  51.0 7.2 %fusion.101 = (f32[4,4,256]{2,1,0:T(4,128)S(1)}, f32[1,4,4,256,1024]{3,4,2,1,0:T(8,128)}) fusion(bf16[1024,4,64,1]{0,2,3,1:T(8,128)(2,1)S(1)} %bitcast.253, bf16[256,4,4,32]{0,3,2,1:T(8,128)(2,1)S(1)} %bitcast.266, bf16[256,4,4,32]{0,3,2,1:T(8,128)(2,1)S(1)} %bitcast.264, pred[256,1024]{0,1:T(8,128)(4,1)S(1)} %fusion.71), kind=kOutput, calls=%fused_computation.198 | convolution fusion | flops 550498304 | bytes 18104320 | tf_op jit(solution)/shard_map/scngd,slnd->sngcl/dot_general | solution.py:56
  58.3 8.0 %fusion.3 = f32[4,4,256]{2,1,0:T(4,128)S(1)} fusion(f32[1,4,4,256,1024]{3,4,2,1,0:T(8,128)} %get-tuple-element.51, f32[4,4,256]{2,1,0:T(4,128)S(1)} %get-tuple-element.50), kind=kLoop, calls=%fused_computation.9 | loop fusion | flops 8384512 | bytes 16809984 | tf_op jit(solution)/shard_map/reduce_sum | solution.py:164
  66.3 7.5 %fusion.60 = bf16[4,64,4,256]{3,1,2,0:T(8,128)(2,1)S(1)} fusion(bf16[1024,4,64,1]{0,2,3,1:T(8,128)(2,1)S(1)} %bitcast.269, f32[4,4,256]{2,1,0:T(4,128)S(1)} %fusion.3, f32[1,4,4,256,1024]{3,4,2,1,0:T(8,128)} %get-tuple-element.51, f32[4,4,256]{2,1,0:T(4,128)S(1)} %get-tuple-element.50), kind=kOutput, calls=%fused_computation.114 | convolution fusion | flops 549715968 | bytes 17858560 | tf_op jit(solution)/shard_map/sngcl,slnd->scngd/dot_general | solution.py:167
  78.4 10.2 %fusion.69 = f32[256,4096]{1,0:T(8,128)} fusion(bf16[4096,2048]{1,0:T(8,128)(2,1)} %param.23, bf16[1,256,2048]{2,1,0:T(8,128)(2,1)S(1)} %copy-done.12), kind=kOutput, calls=%fused_computation.125 | convolution fusion | flops 4294967296 | bytes 22020096 | tf_op jit(solution)/shard_map/dot_general | solution.py:19
  94.5 8.8 %collective-permute-done = bf16[256,2048]{1,0:T(8,128)(2,1)} collective-permute-done((bf16[256,2048]{1,0:T(8,128)(2,1)}, bf16[256,2048]{1,0:T(8,128)(2,1)}, u32[]{:S(2)}, u32[]{:S(2)}) %collective-permute-start) | collective-permute-done | bytes 1048608 | tf_op jit(solution)/shard_map/ppermute | solution.py:68
  106.7 10.8 %fusion.102 = f32[256,4096]{1,0:T(8,128)} fusion(bf16[256,2048]{1,0:T(8,128)(2,1)S(1)} %get-tuple-element.27, bf16[2048,4096]{1,0:T(8,128)(2,1)} %param.21), kind=kOutput, calls=%fused_computation.199 | convolution fusion | flops 4294967296 | bytes 22020096 | tf_op jit(solution)/shard_map/dot_general | solution.py:15
  117.5 6.3 %fusion.103 = f32[256,4096]{1,0:T(8,128)} fusion(bf16[256,2048]{1,0:T(8,128)(2,1)S(1)} %get-tuple-element.27, bf16[2048,4096]{1,0:T(8,128)(2,1)S(1)} %bitcast.296), kind=kOutput, calls=%fused_computation.200 | convolution fusion | flops 4294967296 | bytes 22020096 | tf_op jit(solution)/shard_map/dot_general | solution.py:15
  123.8 13.9 %fusion.42 = f32[256,2048]{1,0:T(8,128)} fusion(bf16[2048,4096]{1,0:T(8,128)(2,1)} %param.21, f32[256,4096]{1,0:T(8,128)} %fusion.102, f32[256,4096]{1,0:T(8,128)} %fusion.69, f32[256,4096]{1,0:T(8,128)} %fusion.103), kind=kOutput, calls=%fused_computation.75 | convolution fusion | flops 4305453056 | bytes 31457280 | tf_op jit(solution)/shard_map/dot_general | solution.py:19
  137.7 11.1 %fusion.30 = bf16[256,2048]{1,0:T(8,128)(2,1)S(1)} fusion(f32[256,2048]{1,0:T(8,128)} %fusion.42, bf16[2048,4096]{1,0:T(8,128)(2,1)} %param.22, f32[256,4096]{1,0:T(8,128)} %fusion.69, f32[256,4096]{1,0:T(8,128)} %fusion.102), kind=kOutput, calls=%fused_computation.61 | convolution fusion | flops 4302307328 | bytes 28311552 | tf_op jit(solution)/shard_map/dot_general | solution.py:19
  148.8 13.0 %convolution_convert_fusion.5 = bf16[256,2048]{1,0:T(8,128)(2,1)S(1)} fusion(bf16[4096,2048]{1,0:T(8,128)(2,1)} %param.23, f32[256,4096]{1,0:T(8,128)} %fusion.103, f32[256,4096]{1,0:T(8,128)} %fusion.102), kind=kOutput, calls=%fused_computation.62 | convolution fusion | flops 4301783040 | bytes 26214400 | tf_op jit(solution)/shard_map/dot_general | solution.py:15
  171.4 10.2 %fusion.21 = f32[1024,1024]{1,0:T(8,128)} fusion(bf16[1024,2048]{1,0:T(8,128)(2,1)S(1)} %constant_dynamic-update-slice_fusion.7, bf16[4096,2048]{1,0:T(8,128)(2,1)} %param.23, s32[]{:T(128)S(6)} %select_n.95), kind=kOutput, calls=%fused_computation.36 | convolution fusion | flops 4294967296 | bytes 12582916 | tf_op jit(solution)/shard_map/dot_general | solution.py:19
  183.1 27.1 %collective-permute-done.10 = bf16[128,2048]{1,0:T(8,128)(2,1)} collective-permute-done((bf16[128,2048]{1,0:T(8,128)(2,1)S(1)}, bf16[128,2048]{1,0:T(8,128)(2,1)}, u32[]{:S(2)}, u32[]{:S(2)}) %collective-permute-start.10) | collective-permute-done | bytes 524320 | tf_op jit(solution)/shard_map/ppermute | solution.py:65
  223.2 15.0 %fusion = (f32[4,4,256]{2,1,0:T(4,128)S(1)}, f32[4,1024,256,4]{2,1,3,0:T(8,128)}) fusion(f32[1,4,4,256,1024]{3,4,2,1,0:T(8,128)} %get-tuple-element.51, f32[4,4,256]{2,1,0:T(4,128)S(1)} %bitcast.285, bf16[1024,4,64,1]{0,2,3,1:T(8,128)(2,1)} %bitcast.268, bf16[256,4,4,64]{0,3,2,1:T(8,128)(2,1)} %bitcast.251), kind=kOutput, calls=%fused_computation.3 | convolution fusion | flops 549449728 | bytes 34635776 | tf_op jit(solution)/shard_map/scngd,slnd->sngcl/dot_general | solution.py:210
  238.2 8.6 %fusion.56 = bf16[4,64,1024]{2,1,0:T(8,128)(2,1)S(1)} fusion(bf16[256,4,4,64]{0,3,2,1:T(8,128)(2,1)S(1)} %bitcast.252, f32[1,4,4,256,1024]{3,4,2,1,0:T(8,128)} %get-tuple-element.51, f32[4,4,256]{2,1,0:T(4,128)S(1)} %bitcast.286), kind=kOutput, calls=%fused_computation.111 | convolution fusion | flops 545521664 | bytes 17842176 | tf_op jit(solution)/shard_map/sngcl,scngd->slnd/dot_general | solution.py:220
  255.7 10.1 %fusion.17 = f32[1024,1024]{1,0:T(8,128)} fusion(bf16[1024,2048]{1,0:T(8,128)(2,1)S(1)} %constant_dynamic-update-slice_fusion, bf16[2048,4096]{1,0:T(8,128)(2,1)} %param.21, s32[]{:T(128)S(6)} %select_n.95), kind=kOutput, calls=%fused_computation.32 | convolution fusion | flops 4294967296 | bytes 12582916 | tf_op jit(solution)/shard_map/dot_general | solution.py:15
  265.8 8.4 %fusion.19 = f32[1024,1024]{1,0:T(8,128)} fusion(bf16[1024,2048]{1,0:T(8,128)(2,1)S(1)} %constant_dynamic-update-slice_fusion, bf16[2048,4096]{1,0:T(8,128)(2,1)} %param.22, s32[]{:T(128)S(6)} %select_n.95), kind=kOutput, calls=%fused_computation.34 | convolution fusion | flops 4294967296 | bytes 12582916 | tf_op jit(solution)/shard_map/dot_general | solution.py:15
  274.3 8.0 %fusion.8 = bf16[4,4,256,1024]{2,3,1,0:T(8,128)(2,1)S(1)} fusion(f32[4,1024,256,4]{2,1,3,0:T(8,128)} %get-tuple-element.53, f32[1,4,4,256,1024]{3,4,2,1,0:T(8,128)S(1)} %bitcast.245, f32[4,4,256]{2,1,0:T(4,128)S(1)} %get-tuple-element.52, f32[4,4,256]{2,1,0:T(4,128)S(1)} %bitcast.287), kind=kLoop, calls=%fused_computation.13 | loop fusion | flops 16777216 | bytes 41975808 | tf_op jit(solution)/shard_map/reshape.27
  294.5 5.2 convolution_convert_fusion.3
  299.8 12.0 %convolution_convert_fusion.4 = bf16[2048,1024]{1,0:T(8,128)(2,1)S(1)} fusion(bf16[1024,2048]{1,0:T(8,128)(2,1)S(1)} %copy-done.42, f32[1024,1024]{1,0:T(8,128)} %fusion.17, f32[1024,1024]{1,0:T(8,128)} %fusion.21, f32[1024,1024]{1,0:T(8,128)} %fusion.19), kind=kOutput, calls=%fused_computation.45 | convolution fusion | flops 4307550208 | bytes 20971520 | tf_op jit(solution)/shard_map/dot_general | solution.py:23
  311.8 10.9 %convolution_convert_fusion.2 = bf16[2048,1024]{1,0:T(8,128)(2,1)S(1)} fusion(bf16[1024,2048]{1,0:T(8,128)(2,1)} %copy-done.45, f32[1024,1024]{1,0:T(8,128)} %fusion.19, f32[1024,1024]{1,0:T(8,128)} %fusion.17), kind=kOutput, calls=%fused_computation.43 | convolution fusion | flops 4303355904 | bytes 16777216 | tf_op jit(solution)/shard_map/dot_general | solution.py:23
  343.9 18.0 %collective-permute-done.7 = bf16[4,1,128,1024]{3,2,0,1:T(8,128)(2,1)S(1)} collective-permute-done((bf16[4,1,128,1024]{3,2,0,1:T(8,128)(2,1)S(1)}, bf16[4,1,128,1024]{3,2,0,1:T(8,128)(2,1)S(1)}, u32[]{:S(2)}, u32[]{:S(2)}) %collective-permute-start.7) | collective-permute-done | bytes 1048608 | tf_op jit(solution)/shard_map/ppermute | solution.py:68
  363.2 5.3 all-to-all-start.1
  376.9 19.6 %collective-permute-done.21 = bf16[4,1,128,1024]{3,2,1,0:T(8,128)(2,1)S(1)} collective-permute-done((bf16[4,1,128,1024]{3,2,1,0:T(8,128)(2,1)S(1)}, bf16[4,1,128,1024]{3,2,1,0:T(8,128)(2,1)S(1)}, u32[]{:S(2)}, u32[]{:S(2)}) %collective-permute-start.21) | collective-permute-done | bytes 1048608 | tf_op jit(solution)/shard_map/ppermute | solution.py:68
  417.9 13.4 %collective-permute-done.23 = bf16[4,1,128,1024]{3,2,1,0:T(8,128)(2,1)S(1)} collective-permute-done((bf16[4,1,128,1024]{3,2,1,0:T(8,128)(2,1)S(1)}, bf16[4,1,128,1024]{3,2,1,0:T(8,128)(2,1)S(1)}, u32[]{:S(2)}, u32[]{:S(2)}) %collective-permute-start.23) | collective-permute-done | bytes 1048608 | tf_op jit(solution)/shard_map/ppermute | solution.py:68
  432.7 5.1 all-to-all-start.3
  447.6 6.3 %collective-permute-done.25 = bf16[4,1,128,1024]{3,2,1,0:T(8,128)(2,1)} collective-permute-done((bf16[4,1,128,1024]{3,2,1,0:T(8,128)(2,1)}, bf16[4,1,128,1024]{3,2,1,0:T(8,128)(2,1)}, u32[]{:S(2)}, u32[]{:S(2)}) %collective-permute-start.25) | collective-permute-done | bytes 1048608 | tf_op jit(solution)/shard_map/ppermute | solution.py:68
  466.5 18.0 %collective-permute-done.5 = bf16[4,1,128,1536]{3,2,1,0:T(8,128)(2,1)} collective-permute-done((bf16[4,1,128,1536]{3,2,1,0:T(8,128)(2,1)}, bf16[4,1,128,1536]{3,2,1,0:T(8,128)(2,1)}, u32[]{:S(2)}, u32[]{:S(2)}) %collective-permute-start.5) | collective-permute-done | bytes 1572896 | tf_op jit(solution)/shard_map/ppermute | solution.py:68
  497.9 57.9 %reduce-scatter.7.cloned.1.call-done = f32[128,2]{1,0:T(8,128)} async-done(((f32[2048,2]{1,0:T(8,128)}), f32[128,2]{1,0:T(8,128)}) %reduce-scatter.7.cloned.1.call-update) | async-done | bytes 1040
  (285 shorter events, 180.7 us)
Async XLA Ops:
  7.2 323.3 %reduce-scatter.5.cloned.1.call-start = ((), (), s32[]{:S(2)}) async-start(), calls=%async_computation.7 | async-start | bytes 1310720 | tf_op jit(solution)/shard_map/reduce_scatter | solution.py:230
  9.3 79.5 %collective-permute-start.14 = (bf16[128,2048]{1,0:T(8,128)(2,1)}, bf16[128,2048]{1,0:T(8,128)(2,1)}, u32[]{:S(2)}, u32[]{:S(2)}) collective-permute-start(bf16[128,2048]{1,0:T(8,128)(2,1)} %dynamic-slice_bitcast_fusion.4), channel_id=1, source_target_pairs={{8,0},{16,8},{24,16},{0,24},{9,1},{17,9},{25,17},{1,25},{10,2},{18... | collective-permute-start | bytes 1572872 | tf_op jit(solution)/shard_map/ppermute | solution.py:65
  14.4 75.0 %collective-permute-start.16 = (bf16[128,2048]{1,0:T(8,128)(2,1)}, bf16[128,2048]{1,0:T(8,128)(2,1)}, u32[]{:S(2)}, u32[]{:S(2)}) collective-permute-start(bf16[128,2048]{1,0:T(8,128)(2,1)} %dynamic-slice_bitcast_fusion.4), channel_id=1, source_target_pairs={{16,0},{24,8},{0,16},{8,24},{17,1},{25,9},{1,17},{9,25},{18,2},{26... | collective-permute-start | bytes 1572872 | tf_op jit(solution)/shard_map/ppermute | solution.py:65
  14.4 76.5 %collective-permute-start.18 = (bf16[128,2048]{1,0:T(8,128)(2,1)}, bf16[128,2048]{1,0:T(8,128)(2,1)}, u32[]{:S(2)}, u32[]{:S(2)}) collective-permute-start(bf16[128,2048]{1,0:T(8,128)(2,1)} %dynamic-slice_bitcast_fusion.4), channel_id=1, source_target_pairs={{24,0},{0,8},{8,16},{16,24},{25,1},{1,9},{9,17},{17,25},{26,2},{2,... | collective-permute-start | bytes 1572872 | tf_op jit(solution)/shard_map/ppermute | solution.py:65
  76.9 26.4 %collective-permute-start = (bf16[256,2048]{1,0:T(8,128)(2,1)}, bf16[256,2048]{1,0:T(8,128)(2,1)}, u32[]{:S(2)}, u32[]{:S(2)}) collective-permute-start(bf16[256,2048]{1,0:T(8,128)(2,1)} %convolution_convert_fusion.6), channel_id=1, source_target_pairs={{0,1},{1,0},{2,3},{3,2},{4,5},{5,4},{6,7},{7,6},{8,9},{9,8},{10,11... | collective-permute-start | bytes 3145736 | tf_op jit(solution)/shard_map/ppermute | solution.py:68
  88.8 77.0 %collective-permute-start.15 = (bf16[128,2048]{1,0:T(8,128)(2,1)}, bf16[128,2048]{1,0:T(8,128)(2,1)}, u32[]{:S(2)}, u32[]{:S(2)}) collective-permute-start(bf16[128,2048]{1,0:T(8,128)(2,1)} %collective-permute-done.14), channel_id=1, source_target_pairs={{1,0},{0,1},{3,2},{2,3},{5,4},{4,5},{7,6},{6,7},{9,8},{8,9},{11,10... | collective-permute-start | bytes 1572872 | tf_op jit(solution)/shard_map/ppermute | solution.py:65
  89.4 78.6 %collective-permute-start.17 = (bf16[128,2048]{1,0:T(8,128)(2,1)}, bf16[128,2048]{1,0:T(8,128)(2,1)S(1)}, u32[]{:S(2)}, u32[]{:S(2)}) collective-permute-start(bf16[128,2048]{1,0:T(8,128)(2,1)} %collective-permute-done.16), channel_id=1, source_target_pairs={{1,0},{0,1},{3,2},{2,3},{5,4},{4,5},{7,6},{6,7},{9,8},{8,9},{11,10... | collective-permute-start | bytes 1572872 | tf_op jit(solution)/shard_map/ppermute | solution.py:65
  90.9 79.8 %collective-permute-start.19 = (bf16[128,2048]{1,0:T(8,128)(2,1)}, bf16[128,2048]{1,0:T(8,128)(2,1)S(1)}, u32[]{:S(2)}, u32[]{:S(2)}) collective-permute-start(bf16[128,2048]{1,0:T(8,128)(2,1)} %collective-permute-done.18), channel_id=1, source_target_pairs={{1,0},{0,1},{3,2},{2,3},{5,4},{4,5},{7,6},{6,7},{9,8},{8,9},{11,10... | collective-permute-start | bytes 1572872 | tf_op jit(solution)/shard_map/ppermute | solution.py:65
  161.8 19.7 %collective-permute-start.8 = (bf16[128,2048]{1,0:T(8,128)(2,1)S(1)}, bf16[128,2048]{1,0:T(8,128)(2,1)}, u32[]{:S(2)}, u32[]{:S(2)}) collective-permute-start(bf16[128,2048]{1,0:T(8,128)(2,1)S(1)} %constant_dynamic-slice_fusion.3), channel_id=1, source_target_pairs={{8,0},{16,8},{24,16},{0,24},{9,1},{17,9},{25,17},{1,25},{10,2},{18... | collective-permute-start | bytes 1572872 | tf_op jit(solution)/shard_map/ppermute | solution.py:65
  164.7 45.6 %collective-permute-start.10 = (bf16[128,2048]{1,0:T(8,128)(2,1)S(1)}, bf16[128,2048]{1,0:T(8,128)(2,1)}, u32[]{:S(2)}, u32[]{:S(2)}) collective-permute-start(bf16[128,2048]{1,0:T(8,128)(2,1)S(1)} %constant_dynamic-slice_fusion.3), channel_id=1, source_target_pairs={{16,0},{24,8},{0,16},{8,24},{17,1},{25,9},{1,17},{9,25},{18,2},{26... | collective-permute-start | bytes 1572872 | tf_op jit(solution)/shard_map/ppermute | solution.py:65
  165.8 46.0 %collective-permute-start.12 = (bf16[128,2048]{1,0:T(8,128)(2,1)S(1)}, bf16[128,2048]{1,0:T(8,128)(2,1)}, u32[]{:S(2)}, u32[]{:S(2)}) collective-permute-start(bf16[128,2048]{1,0:T(8,128)(2,1)S(1)} %constant_dynamic-slice_fusion.3), channel_id=1, source_target_pairs={{24,0},{0,8},{8,16},{16,24},{25,1},{1,9},{9,17},{17,25},{26,2},{2,... | collective-permute-start | bytes 1572872 | tf_op jit(solution)/shard_map/ppermute | solution.py:65
  168.0 46.2 %collective-permute-start.2 = (bf16[256,2048]{1,0:T(8,128)(2,1)S(1)}, bf16[256,2048]{1,0:T(8,128)(2,1)S(1)}, u32[]{:S(2)}, u32[]{:S(2)}) collective-permute-start(bf16[256,2048]{1,0:T(8,128)(2,1)S(1)} %fusion.30), channel_id=1, source_target_pairs={{0,1},{1,0},{2,3},{3,2},{4,5},{5,4},{6,7},{7,6},{8,9},{9,8},{10,11... | collective-permute-start | bytes 3145736 | tf_op jit(solution)/shard_map/ppermute | solution.py:68
  170.7 45.8 %collective-permute-start.1 = (bf16[256,2048]{1,0:T(8,128)(2,1)S(1)}, bf16[256,2048]{1,0:T(8,128)(2,1)S(1)}, u32[]{:S(2)}, u32[]{:S(2)}) collective-permute-start(bf16[256,2048]{1,0:T(8,128)(2,1)S(1)} %convolution_convert_fusion.5), channel_id=1, source_target_pairs={{0,1},{1,0},{2,3},{3,2},{4,5},{5,4},{6,7},{7,6},{8,9},{9,8},{10,11... | collective-permute-start | bytes 3145736 | tf_op jit(solution)/shard_map/ppermute | solution.py:68
  181.6 65.3 %collective-permute-start.9 = (bf16[128,2048]{1,0:T(8,128)(2,1)}, bf16[128,2048]{1,0:T(8,128)(2,1)}, u32[]{:S(2)}, u32[]{:S(2)}) collective-permute-start(bf16[128,2048]{1,0:T(8,128)(2,1)} %collective-permute-done.8), channel_id=1, source_target_pairs={{1,0},{0,1},{3,2},{2,3},{5,4},{4,5},{7,6},{6,7},{9,8},{8,9},{11,10... | collective-permute-start | bytes 1572872 | tf_op jit(solution)/shard_map/ppermute | solution.py:65
  210.3 38.8 %collective-permute-start.11 = (bf16[128,2048]{1,0:T(8,128)(2,1)}, bf16[128,2048]{1,0:T(8,128)(2,1)}, u32[]{:S(2)}, u32[]{:S(2)}) collective-permute-start(bf16[128,2048]{1,0:T(8,128)(2,1)} %collective-permute-done.10), channel_id=1, source_target_pairs={{1,0},{0,1},{3,2},{2,3},{5,4},{4,5},{7,6},{6,7},{9,8},{8,9},{11,10... | collective-permute-start | bytes 1572872 | tf_op jit(solution)/shard_map/ppermute | solution.py:65
  211.8 42.8 %collective-permute-start.13 = (bf16[128,2048]{1,0:T(8,128)(2,1)}, bf16[128,2048]{1,0:T(8,128)(2,1)}, u32[]{:S(2)}, u32[]{:S(2)}) collective-permute-start(bf16[128,2048]{1,0:T(8,128)(2,1)} %collective-permute-done.12), channel_id=1, source_target_pairs={{1,0},{0,1},{3,2},{2,3},{5,4},{4,5},{7,6},{6,7},{9,8},{8,9},{11,10... | collective-permute-start | bytes 1572872 | tf_op jit(solution)/shard_map/ppermute | solution.py:65
  292.4 39.1 %collective-permute-start.6 = (bf16[4,2,128,1024]{3,2,0,1:T(8,128)(2,1)}, bf16[4,2,128,1024]{3,2,0,1:T(8,128)(2,1)S(1)}, u32[]{:S(2)}, u32[]{:S(2)}) collective-permute-start(bf16[4,2,128,1024]{3,2,0,1:T(8,128)(2,1)} %bitcast.239), channel_id=1, source_target_pairs={{0,2},{2,0},{4,6},{6,4},{1,3},{3,1},{5,7},{7,5},{8,10},{10,8},{12,... | collective-permute-start | bytes 6291464 | tf_op jit(solution)/shard_map/ppermute | solution.py:68
  324.4 44.2 %collective-permute-start.20 = (bf16[4,2,128,1024]{3,2,1,0:T(8,128)(2,1)}, bf16[4,2,128,1024]{3,2,1,0:T(8,128)(2,1)}, u32[]{:S(2)}, u32[]{:S(2)}) collective-permute-start(bf16[4,2,128,1024]{3,2,1,0:T(8,128)(2,1)} %dynamic-slice_bitcast_fusion.3), channel_id=1, source_target_pairs={{0,2},{2,0},{4,6},{6,4},{1,3},{3,1},{5,7},{7,5},{8,10},{10,8},{12,... | collective-permute-start | bytes 6291464 | tf_op jit(solution)/shard_map/ppermute | solution.py:68
  325.8 47.2 %collective-permute-start.22 = (bf16[4,2,128,1024]{3,2,1,0:T(8,128)(2,1)}, bf16[4,2,128,1024]{3,2,1,0:T(8,128)(2,1)}, u32[]{:S(2)}, u32[]{:S(2)}) collective-permute-start(bf16[4,2,128,1024]{3,2,1,0:T(8,128)(2,1)} %dynamic-slice_bitcast_fusion.2), channel_id=1, source_target_pairs={{0,2},{2,0},{4,6},{6,4},{1,3},{3,1},{5,7},{7,5},{8,10},{10,8},{12,... | collective-permute-start | bytes 6291464 | tf_op jit(solution)/shard_map/ppermute | solution.py:68
  327.9 82.0 %collective-permute-start.24 = (bf16[4,2,128,1024]{3,2,1,0:T(8,128)(2,1)}, bf16[4,2,128,1024]{3,2,1,0:T(8,128)(2,1)}, u32[]{:S(2)}, u32[]{:S(2)}) collective-permute-start(bf16[4,2,128,1024]{3,2,1,0:T(8,128)(2,1)} %dynamic-slice_bitcast_fusion.1), channel_id=1, source_target_pairs={{0,2},{2,0},{4,6},{6,4},{1,3},{3,1},{5,7},{7,5},{8,10},{10,8},{12,... | collective-permute-start | bytes 6291464 | tf_op jit(solution)/shard_map/ppermute | solution.py:68
  336.2 25.6 %collective-permute-start.7 = (bf16[4,1,128,1024]{3,2,0,1:T(8,128)(2,1)S(1)}, bf16[4,1,128,1024]{3,2,0,1:T(8,128)(2,1)S(1)}, u32[]{:S(2)}, u32[]{:S(2)}) collective-permute-start(bf16[4,1,128,1024]{3,2,0,1:T(8,128)(2,1)S(1)} %constant_dynamic-slice_fusion.4), channel_id=1, source_target_pairs={{0,4},{2,6},{4,0},{6,2},{1,5},{3,7},{5,1},{7,3},{8,12},{10,14},{12... | collective-permute-start | bytes 3145736 | tf_op jit(solution)/shard_map/ppermute | solution.py:68
  343.7 94.2 %collective-permute-start.4 = (bf16[4,2,128,1536]{3,2,1,0:T(8,128)(2,1)}, bf16[4,2,128,1536]{3,2,1,0:T(8,128)(2,1)}, u32[]{:S(2)}, u32[]{:S(2)}) collective-permute-start(bf16[4,2,128,1536]{3,2,1,0:T(8,128)(2,1)} %dynamic-slice_bitcast_fusion), channel_id=1, source_target_pairs={{0,2},{2,0},{4,6},{6,4},{1,3},{3,1},{5,7},{7,5},{8,10},{10,8},{12,... | collective-permute-start | bytes 9437192 | tf_op jit(solution)/shard_map/ppermute | solution.py:68
  363.2 34.7 %all-to-all-start.1 = ((bf16[4,128,1024]{2,1,0:T(8,128)(2,1)}), bf16[4,128,1024]{2,1,0:T(8,128)(2,1)S(1)}, u32[]{:S(2)}, u32[]{:S(2)}) async-start(bf16[4,128,1024]{2,1,0:T(8,128)(2,1)} %fusion.64), calls=%async_computation.2 | async-start | bytes 2097152 | tf_op jit(solution)/shard_map/all_to_all | solution.py:108
  372.1 24.5 %collective-permute-start.21 = (bf16[4,1,128,1024]{3,2,1,0:T(8,128)(2,1)S(1)}, bf16[4,1,128,1024]{3,2,1,0:T(8,128)(2,1)S(1)}, u32[]{:S(2)}, u32[]{:S(2)}) collective-permute-start(bf16[4,1,128,1024]{3,2,1,0:T(8,128)(2,1)S(1)} %constant_dynamic-slice_fusion.2), channel_id=1, source_target_pairs={{0,4},{2,6},{4,0},{6,2},{1,5},{3,7},{5,1},{7,3},{8,12},{10,14},{12... | collective-permute-start | bytes 3145736 | tf_op jit(solution)/shard_map/ppermute | solution.py:68
  398.9 33.8 %all-to-all-start.2 = ((bf16[4,128,1024]{2,1,0:T(8,128)(2,1)}), bf16[4,128,1024]{2,1,0:T(8,128)(2,1)S(1)}, u32[]{:S(2)}, u32[]{:S(2)}) async-start(bf16[4,128,1024]{2,1,0:T(8,128)(2,1)} %fusion.65), calls=%async_computation.3 | async-start | bytes 2097152 | tf_op jit(solution)/shard_map/all_to_all | solution.py:104
  405.2 26.1 %collective-permute-start.23 = (bf16[4,1,128,1024]{3,2,1,0:T(8,128)(2,1)S(1)}, bf16[4,1,128,1024]{3,2,1,0:T(8,128)(2,1)S(1)}, u32[]{:S(2)}, u32[]{:S(2)}) collective-permute-start(bf16[4,1,128,1024]{3,2,1,0:T(8,128)(2,1)S(1)} %constant_dynamic-slice_fusion.1), channel_id=1, source_target_pairs={{0,4},{2,6},{4,0},{6,2},{1,5},{3,7},{5,1},{7,3},{8,12},{10,14},{12... | collective-permute-start | bytes 3145736 | tf_op jit(solution)/shard_map/ppermute | solution.py:68
  415.0 38.9 %collective-permute-start.25 = (bf16[4,1,128,1024]{3,2,1,0:T(8,128)(2,1)}, bf16[4,1,128,1024]{3,2,1,0:T(8,128)(2,1)}, u32[]{:S(2)}, u32[]{:S(2)}) collective-permute-start(bf16[4,1,128,1024]{3,2,1,0:T(8,128)(2,1)} %constant_dynamic-slice_fusion), channel_id=1, source_target_pairs={{0,4},{2,6},{4,0},{6,2},{1,5},{3,7},{5,1},{7,3},{8,12},{10,14},{12... | collective-permute-start | bytes 3145736 | tf_op jit(solution)/shard_map/ppermute | solution.py:68
  432.7 24.7 %all-to-all-start.3 = ((bf16[4,128,1024]{2,1,0:T(8,128)(2,1)}), bf16[4,128,1024]{2,1,0:T(8,128)(2,1)}, u32[]{:S(2)}, u32[]{:S(2)}) async-start(bf16[4,128,1024]{2,1,0:T(8,128)(2,1)} %fusion.66), calls=%async_computation.4 | async-start | bytes 2097152 | tf_op jit(solution)/shard_map/all_to_all | solution.py:104
  444.6 40.0 %collective-permute-start.5 = (bf16[4,1,128,1536]{3,2,1,0:T(8,128)(2,1)}, bf16[4,1,128,1536]{3,2,1,0:T(8,128)(2,1)}, u32[]{:S(2)}, u32[]{:S(2)}) collective-permute-start(bf16[4,1,128,1536]{3,2,1,0:T(8,128)(2,1)} %constant_dynamic-slice_fusion.7), channel_id=1, source_target_pairs={{0,4},{2,6},{4,0},{6,2},{1,5},{3,7},{5,1},{7,3},{8,12},{10,14},{12... | collective-permute-start | bytes 4718600 | tf_op jit(solution)/shard_map/ppermute | solution.py:68
  457.5 30.0 %all-to-all-start.4 = ((bf16[4,128,1024]{2,1,0:T(8,128)(2,1)}), bf16[4,128,1024]{2,1,0:T(8,128)(2,1)}, u32[]{:S(2)}, u32[]{:S(2)}) async-start(bf16[4,128,1024]{2,1,0:T(8,128)(2,1)} %fusion.67), calls=%async_computation.5 | async-start | bytes 2097152 | tf_op jit(solution)/shard_map/all_to_all | solution.py:104
  487.5 82.1 %all-to-all-start = ((bf16[4,128,1536]{2,1,0:T(8,128)(2,1)}), bf16[4,128,1536]{2,1,0:T(8,128)(2,1)}, u32[]{:S(2)}, u32[]{:S(2)}) async-start(bf16[4,128,1536]{2,1,0:T(8,128)(2,1)} %fusion.51), calls=%async_computation.1 | async-start | bytes 3145728 | tf_op jit(solution)/shard_map/all_to_all | solution.py:108
  492.3 63.5 %reduce-scatter.7.cloned.1.call-start = ((), (), s32[]{:S(2)}) async-start(), calls=%async_computation.8 | async-start | bytes 1114112
  (66 other events, 700.6 us)
Sparse Core Ops, SparseCore 0:
  286.9 25.7 reduce-scatter.4
  497.3 58.4 reduce-scatter.6
where the time goes:
time: 585 us; the launch traced here: 580 us
  matrix products  187 us (32%)
  waiting for transfers between devices  174 us (30%)
  local copies, waits for them, and re-layouts  67.7 us (12%)
  other arithmetic  67.5 us (12%)
  starting transfers between devices  51.6 us (9%)
  between operations  16.4 us (3%)
  blocking collectives  15.4 us (3%)
    ppermute x14, waiting for transfers between devices, flip(): return lax.ppermute(v, axis, [(i, i ^ bit) for i in range(n)])  88.3 us
    unnamed x3, waiting for transfers between devices  57.9 us
    dot_general x9, matrix products, dot_plain(): return jnp.dot(left, right, preferred_element_type=F32)  57.9 us
    dot_general x8, matrix products, dot_right(): lax.dot_general(left, right, (((1,), (1,)), ((), ())), preferred_element_...  53.4 us
    unnamed x147, local copies, waits for them, and re-layouts  35.9 us
    dot_general x5, matrix products, dot_left(): lax.dot_general(left, right, (((0,), (0,)), ((), ())), preferred_element_...  33.4 us
    ppermute x12, waiting for transfers between devices, pull(): return lax.ppermute(v, axis, [((i + s) % n, i) for i in range(n)])  27.2 us
    convert_element_type x5, other arithmetic, ctx_sum(): work = (keep.astype(F32) + got.astype(F32)).astype(BF)  17.1 us
  transfers between devices with their start and end apart: 33, of which 11 were waited for; matrix products, arithmetic and copies ran while one was open for 47% of the time, Pallas kernels for 0%

commit v1 on v0

--- a/solution.py
+++ b/solution.py
@@ -9,6 +9,28 @@
 NEG = -1e30
 BF = jnp.bfloat16
 F32 = jnp.float32
+
+
+def cut_along(shard, dim, size):
+    before, after = (shard.shape[:dim], shard.shape[dim + 1 :])
+    return jnp.moveaxis(shard.reshape(*before, size, -1, *after), dim, 0)
+
+
+def laid_out(blocks, dim):
+    blocks = jnp.moveaxis(blocks, 0, dim)
+    dims = blocks.shape
+    return blocks.reshape(*dims[:dim], dims[dim] * dims[dim + 1], *dims[dim + 2 :])
+
+
+def pairwise_exchange(array, axis, split_dim, concat_dim):
+    length, place = (lax.axis_size(axis), lax.axis_index(axis))
+    tiles = cut_along(array, split_dim, length)
+    outs = [tiles[place]]
+    for step in range(1, length):
+        sent = tiles[place ^ step]
+        outs.append(lax.ppermute(sent, axis, [(i, i ^ step) for i in range(length)]))
+    tiles = jnp.stack(outs)[place ^ jnp.arange(length)]
+    return laid_out(tiles, concat_dim)
 
 
 def dot_plain(left, right):
@@ -101,7 +123,7 @@
         return work.reshape(ndp, r, full.shape[1])
 
     def finish_slices(full):
-        got = lax.all_to_all(ctx_sum(full), "dp", 0, 0, tiled=True)
+        got = pairwise_exchange(ctx_sum(full), "dp", 0, 0)
         return jnp.swapaxes(got, 0, 1).reshape(got.shape[1], -1).astype(F32)
 
     def finish_sum(full):

time: 585 us -> 564 us (0.964)
  waiting for transfers between devices: 174 us -> 160 us
    unnamed x3, waiting for transfers between devices: 57.9 us -> 0.03 us
    ppermute x0 -> x9, waiting for transfers between devices: none -> 40.2 us  [pairwise_exchange(): lax.ppermute(sent, axis, [(i, i ^ step) for i in range(length)])]
    ppermute x14, waiting for transfers between devices: 88.3 us -> 120 us  [flip(): return lax.ppermute(v, axis, [(i, i ^ bit) for i in range(n)])]
    ppermute x12, waiting for transfers between devices: 27.2 us -> 0.03 us  [pull(): return lax.ppermute(v, axis, [((i + s) % n, i) for i in range(n)])]
    ppermute x0 -> x9, starting transfers between devices: none -> 15.7 us  [pairwise_exchange(): lax.ppermute(sent, axis, [(i, i ^ step) for i in range(length)])]
    all_to_all x3 -> x0, starting transfers between devices: 14.2 us -> none  [finish_slices(): got = lax.all_to_all(ctx_sum(full), 'dp', 0, 0, tiled=True)]
    unnamed x147 -> x151, local copies, waits for them, and re-layouts: 35.9 us -> 29.9 us
    another operation x5 -> x8, other arithmetic: 8.43 us -> 12.2 us
  transfers between devices with their start and end apart: 33 -> 39, of which waited for: 11 -> 11; matrix products, arithmetic and copies ran while one was open for 47% -> 48% of each run, Pallas kernels for 0% -> 0%
where the time goes in v1:
time: 564 us; the launch traced here: 559 us
  matrix products  184 us (33%)
  waiting for transfers between devices  160 us (28%)
  local copies, waits for them, and re-layouts  65.7 us (12%)
  other arithmetic  64.6 us (11%)
  starting transfers between devices  53.2 us (9%)
  between operations  16.1 us (3%)
  blocking collectives  15.1 us (3%)
    ppermute x14, waiting for transfers between devices, flip(): return lax.ppermute(v, axis, [(i, i ^ bit) for i in range(n)])  120 us
    dot_general x9, matrix products, dot_plain(): return jnp.dot(left, right, preferred_element_type=F32)  57.5 us
    dot_general x8, matrix products, dot_right(): lax.dot_general(left, right, (((1,), (1,)), ((), ())), preferred_element_...  49.3 us
    ppermute x9, waiting for transfers between devices, pairwise_exchange(): lax.ppermute(sent, axis, [(i, i ^ step) for i in range(length)])  40.2 us
    dot_general x5, matrix products, dot_left(): lax.dot_general(left, right, (((0,), (0,)), ((), ())), preferred_element_...  34.8 us
    unnamed x151, local copies, waits for them, and re-layouts  29.9 us
    convert_element_type x8, other arithmetic, ctx_sum(): work = (keep.astype(F32) + got.astype(F32)).astype(BF)  18.1 us
    ppermute x12, starting transfers between devices, pull(): return lax.ppermute(v, axis, [((i + s) % n, i) for i in range(n)])  17.5 us
  transfers between devices with their start and end apart: 39, of which 11 were waited for; matrix products, arithmetic and copies ran while one was open for 48% of the time, Pallas kernels for 0%

profile of v1, /device:TPU:0, one launch (start us, length us, event | category | flops | bytes accessed | tf_op | source)
XLA Modules:
  0.0 559.3 jit_solution(17564749043781112728)
XLA Ops:
  9.3 5.1 collective-permute-start.14
  18.7 7.6 %all-gather = bf16[1024,256]{1,0:T(8,128)(2,1)} all-gather(bf16[256,256]{1,0:T(8,128)(2,1)S(1)} %convolution_convert_fusion.8), channel_id=2, replica_groups=mesh['dp'=4,'ctx'=4,'tensor'=2] {'ctx'}, dimensions={0}, use_global_device_ids=true | all-gather | bytes 655360 | tf_op jit(solution)/shard_map/all_gather | solution.py:172
  31.8 7.5 %all_gather.7 = bf16[1,1024,256]{1,2,0:T(8,128)(2,1)S(1)} all-gather(bf16[1,256,256]{1,2,0:T(8,128)(2,1)S(1)} %bitcast.312), channel_id=1, replica_groups=mesh['dp'=4,'ctx'=4,'tensor'=2] {'ctx'}, dimensions={1}, use_global_device_ids=true | all-gather | bytes 655360 | tf_op jit(solution)/shard_map/all_gather | solution.py:171
  39.3 6.7 %copy.49 = bf16[2048,1024]{0,1:T(8,128)(2,1)} copy(bf16[2048,1024]{1,0:T(8,128)(2,1)} %param.16) | data formatting | bytes 8388608 | tf_op args[4]
  50.7 7.2 %fusion.99 = (f32[4,4,256]{2,1,0:T(4,128)S(1)}, f32[1,4,4,256,1024]{3,4,2,1,0:T(8,128)}) fusion(bf16[1024,4,64,1]{0,2,3,1:T(8,128)(2,1)S(1)} %bitcast.282, bf16[256,4,4,32]{0,3,2,1:T(8,128)(2,1)S(1)} %bitcast.295, bf16[256,4,4,32]{0,3,2,1:T(8,128)(2,1)S(1)} %bitcast.293, pred[256,1024]{0,1:T(8,128)(4,1)S(1)} %fusion.68), kind=kOutput, calls=%fused_computation.216 | convolution fusion | flops 550498304 | bytes 18104320 | tf_op jit(solution)/shard_map/scngd,slnd->sngcl/dot_general | solution.py:78
  58.0 8.0 %fusion.3 = f32[4,4,256]{2,1,0:T(4,128)S(1)} fusion(f32[1,4,4,256,1024]{3,4,2,1,0:T(8,128)} %get-tuple-element.63, f32[4,4,256]{2,1,0:T(4,128)S(1)} %get-tuple-element.62), kind=kLoop, calls=%fused_computation.12 | loop fusion | flops 8384512 | bytes 16809984 | tf_op jit(solution)/shard_map/reduce_sum | solution.py:186
  66.0 7.5 %fusion.60 = bf16[4,64,4,256]{3,1,2,0:T(8,128)(2,1)S(1)} fusion(bf16[1024,4,64,1]{0,2,3,1:T(8,128)(2,1)S(1)} %bitcast.298, f32[4,4,256]{2,1,0:T(4,128)S(1)} %fusion.3, f32[1,4,4,256,1024]{3,4,2,1,0:T(8,128)} %get-tuple-element.63, f32[4,4,256]{2,1,0:T(4,128)S(1)} %get-tuple-element.62), kind=kOutput, calls=%fused_computation.117 | convolution fusion | flops 549715968 | bytes 17858560 | tf_op jit(solution)/shard_map/sngcl,slnd->scngd/dot_general | solution.py:189
  78.1 10.2 %fusion.66 = f32[256,4096]{1,0:T(8,128)} fusion(bf16[4096,2048]{1,0:T(8,128)(2,1)} %param.23, bf16[1,256,2048]{2,1,0:T(8,128)(2,1)S(1)} %copy-done.14), kind=kOutput, calls=%fused_computation.128 | convolution fusion | flops 4294967296 | bytes 22020096 | tf_op jit(solution)/shard_map/dot_general | solution.py:41
  94.7 8.2 %collective-permute-done = bf16[256,2048]{1,0:T(8,128)(2,1)} collective-permute-done((bf16[256,2048]{1,0:T(8,128)(2,1)}, bf16[256,2048]{1,0:T(8,128)(2,1)}, u32[]{:S(2)}, u32[]{:S(2)}) %collective-permute-start) | collective-permute-done | bytes 1048608 | tf_op jit(solution)/shard_map/ppermute | solution.py:90
  110.8 10.2 %fusion.100 = f32[256,4096]{1,0:T(8,128)} fusion(bf16[256,2048]{1,0:T(8,128)(2,1)S(1)} %get-tuple-element.27, bf16[2048,4096]{1,0:T(8,128)(2,1)} %param.21), kind=kOutput, calls=%fused_computation.217 | convolution fusion | flops 4294967296 | bytes 22020096 | tf_op jit(solution)/shard_map/dot_general | solution.py:37
  121.1 6.2 %fusion.101 = f32[256,4096]{1,0:T(8,128)} fusion(bf16[256,2048]{1,0:T(8,128)(2,1)S(1)} %get-tuple-element.27, bf16[2048,4096]{1,0:T(8,128)(2,1)S(1)} %bitcast.325), kind=kOutput, calls=%fused_computation.218 | convolution fusion | flops 4294967296 | bytes 22020096 | tf_op jit(solution)/shard_map/dot_general | solution.py:37
  127.3 13.9 %fusion.42 = f32[256,2048]{1,0:T(8,128)} fusion(bf16[2048,4096]{1,0:T(8,128)(2,1)} %param.21, f32[256,4096]{1,0:T(8,128)} %fusion.100, f32[256,4096]{1,0:T(8,128)} %fusion.66, f32[256,4096]{1,0:T(8,128)} %fusion.101), kind=kOutput, calls=%fused_computation.78 | convolution fusion | flops 4305453056 | bytes 31457280 | tf_op jit(solution)/shard_map/dot_general | solution.py:41
  141.2 11.1 %fusion.30 = bf16[256,2048]{1,0:T(8,128)(2,1)S(1)} fusion(f32[256,2048]{1,0:T(8,128)} %fusion.42, bf16[2048,4096]{1,0:T(8,128)(2,1)} %param.22, f32[256,4096]{1,0:T(8,128)} %fusion.66, f32[256,4096]{1,0:T(8,128)} %fusion.100), kind=kOutput, calls=%fused_computation.64 | convolution fusion | flops 4302307328 | bytes 28311552 | tf_op jit(solution)/shard_map/dot_general | solution.py:41
  152.3 13.0 %convolution_convert_fusion.5 = bf16[256,2048]{1,0:T(8,128)(2,1)S(1)} fusion(bf16[4096,2048]{1,0:T(8,128)(2,1)} %param.23, f32[256,4096]{1,0:T(8,128)} %fusion.101, f32[256,4096]{1,0:T(8,128)} %fusion.100), kind=kOutput, calls=%fused_computation.65 | convolution fusion | flops 4301783040 | bytes 26214400 | tf_op jit(solution)/shard_map/dot_general | solution.py:37
  170.6 9.8 %fusion.21 = f32[1024,1024]{1,0:T(8,128)} fusion(bf16[1024,2048]{1,0:T(8,128)(2,1)S(1)} %constant_dynamic-update-slice_fusion.7, bf16[4096,2048]{1,0:T(8,128)(2,1)} %param.23, s32[]{:T(128)S(6)} %select_n.127), kind=kOutput, calls=%fused_computation.39 | convolution fusion | flops 4294967296 | bytes 12582916 | tf_op jit(solution)/shard_map/dot_general | solution.py:41
  185.8 7.5 %collective-permute-done.2 = bf16[256,2048]{1,0:T(8,128)(2,1)S(1)} collective-permute-done((bf16[256,2048]{1,0:T(8,128)(2,1)S(1)}, bf16[256,2048]{1,0:T(8,128)(2,1)S(1)}, u32[]{:S(2)}, u32[]{:S(2)}) %collective-permute-start.2) | collective-permute-done | bytes 1048608 | tf_op jit(solution)/shard_map/ppermute | solution.py:90
  194.2 21.6 %collective-permute-done.1 = bf16[256,2048]{1,0:T(8,128)(2,1)S(1)} collective-permute-done((bf16[256,2048]{1,0:T(8,128)(2,1)S(1)}, bf16[256,2048]{1,0:T(8,128)(2,1)S(1)}, u32[]{:S(2)}, u32[]{:S(2)}) %collective-permute-start.1) | collective-permute-done | bytes 1048608 | tf_op jit(solution)/shard_map/ppermute | solution.py:90
  222.5 15.0 %fusion = (f32[4,4,256]{2,1,0:T(4,128)S(1)}, f32[4,1024,256,4]{2,1,3,0:T(8,128)}) fusion(f32[1,4,4,256,1024]{3,4,2,1,0:T(8,128)} %get-tuple-element.63, f32[4,4,256]{2,1,0:T(4,128)S(1)} %bitcast.314, bf16[1024,4,64,1]{0,2,3,1:T(8,128)(2,1)} %bitcast.297, bf16[256,4,4,64]{0,3,2,1:T(8,128)(2,1)} %bitcast.280), kind=kOutput, calls=%fused_computation.6 | convolution fusion | flops 549449728 | bytes 34635776 | tf_op jit(solution)/shard_map/scngd,slnd->sngcl/dot_general | solution.py:232
  237.5 8.6 %fusion.56 = bf16[4,64,1024]{2,1,0:T(8,128)(2,1)S(1)} fusion(bf16[256,4,4,64]{0,3,2,1:T(8,128)(2,1)S(1)} %bitcast.281, f32[1,4,4,256,1024]{3,4,2,1,0:T(8,128)} %get-tuple-element.63, f32[4,4,256]{2,1,0:T(4,128)S(1)} %bitcast.315), kind=kOutput, calls=%fused_computation.114 | convolution fusion | flops 545521664 | bytes 17842176 | tf_op jit(solution)/shard_map/sngcl,scngd->slnd/dot_general | solution.py:242
  251.6 10.4 %fusion.17 = f32[1024,1024]{1,0:T(8,128)} fusion(bf16[1024,2048]{1,0:T(8,128)(2,1)S(1)} %constant_dynamic-update-slice_fusion, bf16[2048,4096]{1,0:T(8,128)(2,1)} %param.21, s32[]{:T(128)S(6)} %select_n.127), kind=kOutput, calls=%fused_computation.35 | convolution fusion | flops 4294967296 | bytes 12582916 | tf_op jit(solution)/shard_map/dot_general | solution.py:37
  262.0 8.4 %fusion.19 = f32[1024,1024]{1,0:T(8,128)} fusion(bf16[1024,2048]{1,0:T(8,128)(2,1)S(1)} %constant_dynamic-update-slice_fusion, bf16[2048,4096]{1,0:T(8,128)(2,1)} %param.22, s32[]{:T(128)S(6)} %select_n.127), kind=kOutput, calls=%fused_computation.37 | convolution fusion | flops 4294967296 | bytes 12582916 | tf_op jit(solution)/shard_map/dot_general | solution.py:37
  270.4 8.0 %fusion.8 = bf16[4,4,256,1024]{2,3,1,0:T(8,128)(2,1)S(1)} fusion(f32[4,1024,256,4]{2,1,3,0:T(8,128)} %get-tuple-element.65, f32[1,4,4,256,1024]{3,4,2,1,0:T(8,128)S(1)} %bitcast.274, f32[4,4,256]{2,1,0:T(4,128)S(1)} %get-tuple-element.64, f32[4,4,256]{2,1,0:T(4,128)S(1)} %bitcast.316), kind=kLoop, calls=%fused_computation.16 | loop fusion | flops 16777216 | bytes 41975808 | tf_op jit(solution)/shard_map/reshape.27
  283.0 9.5 %convolution_convert_fusion.3 = bf16[2048,1024]{1,0:T(8,128)(2,1)S(1)} fusion(bf16[1024,2048]{1,0:T(8,128)(2,1)} %copy-done.44, f32[1024,1024]{1,0:T(8,128)} %fusion.21, f32[1024,1024]{1,0:T(8,128)} %fusion.17), kind=kOutput, calls=%fused_computation.47 | convolution fusion | flops 4303355904 | bytes 16777216 | tf_op jit(solution)/shard_map/dot_general | solution.py:45
  292.5 11.6 %convolution_convert_fusion.4 = bf16[2048,1024]{1,0:T(8,128)(2,1)S(1)} fusion(bf16[1024,2048]{1,0:T(8,128)(2,1)S(1)} %copy-done.45, f32[1024,1024]{1,0:T(8,128)} %fusion.17, f32[1024,1024]{1,0:T(8,128)} %fusion.21, f32[1024,1024]{1,0:T(8,128)} %fusion.19), kind=kOutput, calls=%fused_computation.48 | convolution fusion | flops 4307550208 | bytes 20971520 | tf_op jit(solution)/shard_map/dot_general | solution.py:45
  304.1 10.4 %convolution_convert_fusion.2 = bf16[2048,1024]{1,0:T(8,128)(2,1)S(1)} fusion(bf16[1024,2048]{1,0:T(8,128)(2,1)S(1)} %copy-done.49, f32[1024,1024]{1,0:T(8,128)} %fusion.19, f32[1024,1024]{1,0:T(8,128)} %fusion.17), kind=kOutput, calls=%fused_computation.46 | convolution fusion | flops 4303355904 | bytes 16777216 | tf_op jit(solution)/shard_map/dot_general | solution.py:45
  375.5 13.6 %collective-permute-done.21 = bf16[4,1,128,1024]{3,2,1,0:T(8,128)(2,1)} collective-permute-done((bf16[4,1,128,1024]{3,2,1,0:T(8,128)(2,1)}, bf16[4,1,128,1024]{3,2,1,0:T(8,128)(2,1)}, u32[]{:S(2)}, u32[]{:S(2)}) %collective-permute-start.21) | collective-permute-done | bytes 1048608 | tf_op jit(solution)/shard_map/ppermute | solution.py:90
  395.2 19.3 %collective-permute-done.26 = bf16[4,1,128,1024]{3,2,1,0:T(8,128)(2,1)} collective-permute-done((bf16[4,1,128,1024]{3,2,1,0:T(8,128)(2,1)}, bf16[4,1,128,1024]{3,2,1,0:T(8,128)(2,1)}, u32[]{:S(2)}, u32[]{:S(2)}) %collective-permute-start.26) | collective-permute-done | bytes 1048608 | tf_op jit(solution)/shard_map/ppermute | solution.py:90
  418.6 19.0 %collective-permute-done.31 = bf16[4,1,128,1024]{3,2,1,0:T(8,128)(2,1)} collective-permute-done((bf16[4,1,128,1024]{3,2,1,0:T(8,128)(2,1)}, bf16[4,1,128,1024]{3,2,1,0:T(8,128)(2,1)}, u32[]{:S(2)}, u32[]{:S(2)}) %collective-permute-start.31) | collective-permute-done | bytes 1048608 | tf_op jit(solution)/shard_map/ppermute | solution.py:90
  443.3 26.8 %collective-permute-done.5 = bf16[4,1,128,1536]{3,2,1,0:T(8,128)(2,1)} collective-permute-done((bf16[4,1,128,1536]{3,2,1,0:T(8,128)(2,1)}, bf16[4,1,128,1536]{3,2,1,0:T(8,128)(2,1)}, u32[]{:S(2)}, u32[]{:S(2)}) %collective-permute-start.5) | collective-permute-done | bytes 1572896 | tf_op jit(solution)/shard_map/ppermute | solution.py:90
  496.4 14.9 %collective-permute-done.27 = bf16[1,128,1024]{2,1,0:T(8,128)(2,1)} collective-permute-done((bf16[1,128,1024]{2,1,0:T(8,128)(2,1)}, bf16[1,128,1024]{2,1,0:T(8,128)(2,1)}, u32[]{:S(2)}, u32[]{:S(2)}) %collective-permute-start.27) | collective-permute-done | bytes 262176 | tf_op jit(solution)/shard_map/ppermute | solution.py:31
  515.0 6.2 %collective-permute-done.34 = bf16[1,128,1024]{2,1,0:T(8,128)(2,1)} collective-permute-done((bf16[1,128,1024]{2,1,0:T(8,128)(2,1)}, bf16[1,128,1024]{2,1,0:T(8,128)(2,1)}, u32[]{:S(2)}, u32[]{:S(2)}) %collective-permute-start.34) | collective-permute-done | bytes 262176 | tf_op jit(solution)/shard_map/ppermute | solution.py:31
  521.1 19.2 %collective-permute-done.33 = bf16[1,128,1024]{2,1,0:T(8,128)(2,1)} collective-permute-done((bf16[1,128,1024]{2,1,0:T(8,128)(2,1)}, bf16[1,128,1024]{2,1,0:T(8,128)(2,1)}, u32[]{:S(2)}, u32[]{:S(2)}) %collective-permute-start.33) | collective-permute-done | bytes 262176 | tf_op jit(solution)/shard_map/ppermute | solution.py:31
  (312 shorter events, 181.0 us)
Async XLA Ops:
  7.2 319.6 %reduce-scatter.5.cloned.1.call-start = ((), (), s32[]{:S(2)}) async-start(), calls=%async_computation.4 | async-start | bytes 1310720 | tf_op jit(solution)/shard_map/reduce_scatter | solution.py:252
  9.3 79.7 %collective-permute-start.14 = (bf16[128,2048]{1,0:T(8,128)(2,1)}, bf16[128,2048]{1,0:T(8,128)(2,1)}, u32[]{:S(2)}, u32[]{:S(2)}) collective-permute-start(bf16[128,2048]{1,0:T(8,128)(2,1)} %dynamic-slice_bitcast_fusion.4), channel_id=1, source_target_pairs={{8,0},{16,8},{24,16},{0,24},{9,1},{17,9},{25,17},{1,25},{10,2},{18... | collective-permute-start | bytes 1572872 | tf_op jit(solution)/shard_map/ppermute | solution.py:87
  14.4 75.2 %collective-permute-start.16 = (bf16[128,2048]{1,0:T(8,128)(2,1)}, bf16[128,2048]{1,0:T(8,128)(2,1)}, u32[]{:S(2)}, u32[]{:S(2)}) collective-permute-start(bf16[128,2048]{1,0:T(8,128)(2,1)} %dynamic-slice_bitcast_fusion.4), channel_id=1, source_target_pairs={{16,0},{24,8},{0,16},{8,24},{17,1},{25,9},{1,17},{9,25},{18,2},{26... | collective-permute-start | bytes 1572872 | tf_op jit(solution)/shard_map/ppermute | solution.py:87
  14.4 76.7 %collective-permute-start.18 = (bf16[128,2048]{1,0:T(8,128)(2,1)}, bf16[128,2048]{1,0:T(8,128)(2,1)}, u32[]{:S(2)}, u32[]{:S(2)}) collective-permute-start(bf16[128,2048]{1,0:T(8,128)(2,1)} %dynamic-slice_bitcast_fusion.4), channel_id=1, source_target_pairs={{24,0},{0,8},{8,16},{16,24},{25,1},{1,9},{9,17},{17,25},{26,2},{2,... | collective-permute-start | bytes 1572872 | tf_op jit(solution)/shard_map/ppermute | solution.py:87
  76.6 26.4 %collective-permute-start = (bf16[256,2048]{1,0:T(8,128)(2,1)}, bf16[256,2048]{1,0:T(8,128)(2,1)}, u32[]{:S(2)}, u32[]{:S(2)}) collective-permute-start(bf16[256,2048]{1,0:T(8,128)(2,1)} %convolution_convert_fusion.6), channel_id=1, source_target_pairs={{0,1},{1,0},{2,3},{3,2},{4,5},{5,4},{6,7},{7,6},{8,9},{9,8},{10,11... | collective-permute-start | bytes 3145736 | tf_op jit(solution)/shard_map/ppermute | solution.py:90
  89.0 76.3 %collective-permute-start.15 = (bf16[128,2048]{1,0:T(8,128)(2,1)}, bf16[128,2048]{1,0:T(8,128)(2,1)S(1)}, u32[]{:S(2)}, u32[]{:S(2)}) collective-permute-start(bf16[128,2048]{1,0:T(8,128)(2,1)} %collective-permute-done.14), channel_id=1, source_target_pairs={{1,0},{0,1},{3,2},{2,3},{5,4},{4,5},{7,6},{6,7},{9,8},{8,9},{11,10... | collective-permute-start | bytes 1572872 | tf_op jit(solution)/shard_map/ppermute | solution.py:87
  89.6 77.7 %collective-permute-start.17 = (bf16[128,2048]{1,0:T(8,128)(2,1)}, bf16[128,2048]{1,0:T(8,128)(2,1)S(1)}, u32[]{:S(2)}, u32[]{:S(2)}) collective-permute-start(bf16[128,2048]{1,0:T(8,128)(2,1)} %collective-permute-done.16), channel_id=1, source_target_pairs={{1,0},{0,1},{3,2},{2,3},{5,4},{4,5},{7,6},{6,7},{9,8},{8,9},{11,10... | collective-permute-start | bytes 1572872 | tf_op jit(solution)/shard_map/ppermute | solution.py:87
  91.1 78.9 %collective-permute-start.19 = (bf16[128,2048]{1,0:T(8,128)(2,1)}, bf16[128,2048]{1,0:T(8,128)(2,1)S(1)}, u32[]{:S(2)}, u32[]{:S(2)}) collective-permute-start(bf16[128,2048]{1,0:T(8,128)(2,1)} %collective-permute-done.18), channel_id=1, source_target_pairs={{1,0},{0,1},{3,2},{2,3},{5,4},{4,5},{7,6},{6,7},{9,8},{8,9},{11,10... | collective-permute-start | bytes 1572872 | tf_op jit(solution)/shard_map/ppermute | solution.py:87
  106.4 73.9 %collective-permute-start.8 = (bf16[128,2048]{1,0:T(8,128)(2,1)S(1)}, bf16[128,2048]{1,0:T(8,128)(2,1)}, u32[]{:S(2)}, u32[]{:S(2)}) collective-permute-start(bf16[128,2048]{1,0:T(8,128)(2,1)S(1)} %constant_dynamic-slice_fusion.6), channel_id=1, source_target_pairs={{8,0},{16,8},{24,16},{0,24},{9,1},{17,9},{25,17},{1,25},{10,2},{18... | collective-permute-start | bytes 1572872 | tf_op jit(solution)/shard_map/ppermute | solution.py:87
  109.7 72.2 %collective-permute-start.10 = (bf16[128,2048]{1,0:T(8,128)(2,1)S(1)}, bf16[128,2048]{1,0:T(8,128)(2,1)}, u32[]{:S(2)}, u32[]{:S(2)}) collective-permute-start(bf16[128,2048]{1,0:T(8,128)(2,1)S(1)} %constant_dynamic-slice_fusion.6), channel_id=1, source_target_pairs={{16,0},{24,8},{0,16},{8,24},{17,1},{25,9},{1,17},{9,25},{18,2},{26... | collective-permute-start | bytes 1572872 | tf_op jit(solution)/shard_map/ppermute | solution.py:87
  170.0 45.9 %collective-permute-start.1 = (bf16[256,2048]{1,0:T(8,128)(2,1)S(1)}, bf16[256,2048]{1,0:T(8,128)(2,1)S(1)}, u32[]{:S(2)}, u32[]{:S(2)}) collective-permute-start(bf16[256,2048]{1,0:T(8,128)(2,1)S(1)} %convolution_convert_fusion.5), channel_id=1, source_target_pairs={{0,1},{1,0},{2,3},{3,2},{4,5},{5,4},{6,7},{7,6},{8,9},{9,8},{10,11... | collective-permute-start | bytes 3145736 | tf_op jit(solution)/shard_map/ppermute | solution.py:90
  180.3 65.8 %collective-permute-start.9 = (bf16[128,2048]{1,0:T(8,128)(2,1)}, bf16[128,2048]{1,0:T(8,128)(2,1)}, u32[]{:S(2)}, u32[]{:S(2)}) collective-permute-start(bf16[128,2048]{1,0:T(8,128)(2,1)} %collective-permute-done.8), channel_id=1, source_target_pairs={{1,0},{0,1},{3,2},{2,3},{5,4},{4,5},{7,6},{6,7},{9,8},{8,9},{11,10... | collective-permute-start | bytes 1572872 | tf_op jit(solution)/shard_map/ppermute | solution.py:87
  181.9 66.3 %collective-permute-start.11 = (bf16[128,2048]{1,0:T(8,128)(2,1)}, bf16[128,2048]{1,0:T(8,128)(2,1)}, u32[]{:S(2)}, u32[]{:S(2)}) collective-permute-start(bf16[128,2048]{1,0:T(8,128)(2,1)} %collective-permute-done.10), channel_id=1, source_target_pairs={{1,0},{0,1},{3,2},{2,3},{5,4},{4,5},{7,6},{6,7},{9,8},{8,9},{11,10... | collective-permute-start | bytes 1572872 | tf_op jit(solution)/shard_map/ppermute | solution.py:87
  182.4 68.0 %collective-permute-start.13 = (bf16[128,2048]{1,0:T(8,128)(2,1)}, bf16[128,2048]{1,0:T(8,128)(2,1)}, u32[]{:S(2)}, u32[]{:S(2)}) collective-permute-start(bf16[128,2048]{1,0:T(8,128)(2,1)} %collective-permute-done.12), channel_id=1, source_target_pairs={{1,0},{0,1},{3,2},{2,3},{5,4},{4,5},{7,6},{6,7},{9,8},{8,9},{11,10... | collective-permute-start | bytes 1572872 | tf_op jit(solution)/shard_map/ppermute | solution.py:87
  282.9 201.0 %reduce-scatter.7.cloned.1.call-start = ((), (), s32[]{:S(2)}) async-start(), calls=%async_computation.5 | async-start | bytes 1114112
  324.4 26.2 %collective-permute-start.30 = (bf16[4,2,128,1024]{3,2,1,0:T(8,128)(2,1)}, bf16[4,2,128,1024]{3,2,1,0:T(8,128)(2,1)}, u32[]{:S(2)}, u32[]{:S(2)}) collective-permute-start(bf16[4,2,128,1024]{3,2,1,0:T(8,128)(2,1)} %dynamic-slice_bitcast_fusion.1), channel_id=1, source_target_pairs={{0,2},{2,0},{4,6},{6,4},{1,3},{3,1},{5,7},{7,5},{8,10},{10,8},{12,... | collective-permute-start | bytes 6291464 | tf_op jit(solution)/shard_map/ppermute | solution.py:90
  330.1 31.6 %collective-permute-start.4 = (bf16[4,2,128,1536]{3,2,1,0:T(8,128)(2,1)S(1)}, bf16[4,2,128,1536]{3,2,1,0:T(8,128)(2,1)S(1)}, u32[]{:S(2)}, u32[]{:S(2)}) collective-permute-start(bf16[4,2,128,1536]{3,2,1,0:T(8,128)(2,1)S(1)} %dynamic-slice_bitcast_fusion), channel_id=1, source_target_pairs={{0,2},{2,0},{4,6},{6,4},{1,3},{3,1},{5,7},{7,5},{8,10},{10,8},{12,... | collective-permute-start | bytes 9437192 | tf_op jit(solution)/shard_map/ppermute | solution.py:90
  340.3 27.9 %collective-permute-start.7 = (bf16[4,1,128,1024]{3,2,0,1:T(8,128)(2,1)}, bf16[4,1,128,1024]{3,2,0,1:T(8,128)(2,1)}, u32[]{:S(2)}, u32[]{:S(2)}) collective-permute-start(bf16[4,1,128,1024]{3,2,0,1:T(8,128)(2,1)} %constant_dynamic-slice_fusion.7), channel_id=1, source_target_pairs={{0,4},{2,6},{4,0},{6,2},{1,5},{3,7},{5,1},{7,3},{8,12},{10,14},{12... | collective-permute-start | bytes 3145736 | tf_op jit(solution)/shard_map/ppermute | solution.py:90
  345.8 43.4 %collective-permute-start.21 = (bf16[4,1,128,1024]{3,2,1,0:T(8,128)(2,1)}, bf16[4,1,128,1024]{3,2,1,0:T(8,128)(2,1)}, u32[]{:S(2)}, u32[]{:S(2)}) collective-permute-start(bf16[4,1,128,1024]{3,2,1,0:T(8,128)(2,1)} %constant_dynamic-slice_fusion.5), channel_id=1, source_target_pairs={{0,4},{2,6},{4,0},{6,2},{1,5},{3,7},{5,1},{7,3},{8,12},{10,14},{12... | collective-permute-start | bytes 3145736 | tf_op jit(solution)/shard_map/ppermute | solution.py:90
  351.1 63.3 %collective-permute-start.26 = (bf16[4,1,128,1024]{3,2,1,0:T(8,128)(2,1)}, bf16[4,1,128,1024]{3,2,1,0:T(8,128)(2,1)}, u32[]{:S(2)}, u32[]{:S(2)}) collective-permute-start(bf16[4,1,128,1024]{3,2,1,0:T(8,128)(2,1)} %constant_dynamic-slice_fusion.3), channel_id=1, source_target_pairs={{0,4},{2,6},{4,0},{6,2},{1,5},{3,7},{5,1},{7,3},{8,12},{10,14},{12... | collective-permute-start | bytes 3145736 | tf_op jit(solution)/shard_map/ppermute | solution.py:90
  360.0 77.6 %collective-permute-start.31 = (bf16[4,1,128,1024]{3,2,1,0:T(8,128)(2,1)}, bf16[4,1,128,1024]{3,2,1,0:T(8,128)(2,1)}, u32[]{:S(2)}, u32[]{:S(2)}) collective-permute-start(bf16[4,1,128,1024]{3,2,1,0:T(8,128)(2,1)} %constant_dynamic-slice_fusion.1), channel_id=1, source_target_pairs={{0,4},{2,6},{4,0},{6,2},{1,5},{3,7},{5,1},{7,3},{8,12},{10,14},{12... | collective-permute-start | bytes 3145736 | tf_op jit(solution)/shard_map/ppermute | solution.py:90
  365.6 104.5 %collective-permute-start.5 = (bf16[4,1,128,1536]{3,2,1,0:T(8,128)(2,1)}, bf16[4,1,128,1536]{3,2,1,0:T(8,128)(2,1)}, u32[]{:S(2)}, u32[]{:S(2)}) collective-permute-start(bf16[4,1,128,1536]{3,2,1,0:T(8,128)(2,1)} %constant_dynamic-slice_fusion.10), channel_id=1, source_target_pairs={{0,4},{2,6},{4,0},{6,2},{1,5},{3,7},{5,1},{7,3},{8,12},{10,14},{12... | collective-permute-start | bytes 4718600 | tf_op jit(solution)/shard_map/ppermute | solution.py:90
  371.2 103.4 %all-to-all-start.1 = ((bf16[4,128,1024]{2,1,0:T(8,128)(2,1)}), bf16[4,128,1024]{2,1,0:T(8,128)(2,1)}, u32[]{:S(2)}, u32[]{:S(2)}) async-start(bf16[4,128,1024]{2,1,0:T(8,128)(2,1)} %fusion.64), calls=%async_computation.2 | async-start | bytes 2097152 | tf_op jit(solution)/shard_map/all_to_all | solution.py:130
  392.1 94.0 %collective-permute-start.24 = (bf16[1,128,1024]{2,1,0:T(8,128)(2,1)}, bf16[1,128,1024]{2,1,0:T(8,128)(2,1)}, u32[]{:S(2)}, u32[]{:S(2)}) collective-permute-start(bf16[1,128,1024]{2,1,0:T(8,128)(2,1)} %get-tuple-element.47), channel_id=1, source_target_pairs={{0,24},{8,16},{16,8},{24,0},{1,25},{9,17},{17,9},{25,1},{2,26},{10... | collective-permute-start | bytes 786440 | tf_op jit(solution)/shard_map/ppermute | solution.py:31
  395.2 93.0 %collective-permute-start.23 = (bf16[1,128,1024]{2,1,0:T(8,128)(2,1)}, bf16[1,128,1024]{2,1,0:T(8,128)(2,1)}, u32[]{:S(2)}, u32[]{:S(2)}) collective-permute-start(bf16[1,128,1024]{2,1,0:T(8,128)(2,1)} %get-tuple-element.48), channel_id=1, source_target_pairs={{0,16},{8,24},{16,0},{24,8},{1,17},{9,25},{17,1},{25,9},{2,18},{10... | collective-permute-start | bytes 786440 | tf_op jit(solution)/shard_map/ppermute | solution.py:31
  414.4 76.0 %collective-permute-start.22 = (bf16[1,128,1024]{2,1,0:T(8,128)(2,1)}, bf16[1,128,1024]{2,1,0:T(8,128)(2,1)}, u32[]{:S(2)}, u32[]{:S(2)}) collective-permute-start(bf16[1,128,1024]{2,1,0:T(8,128)(2,1)} %get-tuple-element.49), channel_id=1, source_target_pairs={{0,8},{8,0},{16,24},{24,16},{1,9},{9,1},{17,25},{25,17},{2,10},{10... | collective-permute-start | bytes 786440 | tf_op jit(solution)/shard_map/ppermute | solution.py:31
  437.6 56.7 %collective-permute-start.29 = (bf16[1,128,1024]{2,1,0:T(8,128)(2,1)}, bf16[1,128,1024]{2,1,0:T(8,128)(2,1)}, u32[]{:S(2)}, u32[]{:S(2)}) collective-permute-start(bf16[1,128,1024]{2,1,0:T(8,128)(2,1)} %get-tuple-element.43), channel_id=1, source_target_pairs={{0,24},{8,16},{16,8},{24,0},{1,25},{9,17},{17,9},{25,1},{2,26},{10... | collective-permute-start | bytes 786440 | tf_op jit(solution)/shard_map/ppermute | solution.py:31
  470.1 26.3 %collective-permute-start.28 = (bf16[1,128,1024]{2,1,0:T(8,128)(2,1)}, bf16[1,128,1024]{2,1,0:T(8,128)(2,1)}, u32[]{:S(2)}, u32[]{:S(2)}) collective-permute-start(bf16[1,128,1024]{2,1,0:T(8,128)(2,1)} %get-tuple-element.44), channel_id=1, source_target_pairs={{0,16},{8,24},{16,0},{24,8},{1,17},{9,25},{17,1},{25,9},{2,18},{10... | collective-permute-start | bytes 786440 | tf_op jit(solution)/shard_map/ppermute | solution.py:31
  474.6 74.4 %all-to-all-start = ((bf16[4,128,1536]{2,1,0:T(8,128)(2,1)}), bf16[4,128,1536]{2,1,0:T(8,128)(2,1)}, u32[]{:S(2)}, u32[]{:S(2)}) async-start(bf16[4,128,1536]{2,1,0:T(8,128)(2,1)} %fusion.51), calls=%async_computation.1 | async-start | bytes 3145728 | tf_op jit(solution)/shard_map/all_to_all | solution.py:130
  488.2 32.9 %collective-permute-start.34 = (bf16[1,128,1024]{2,1,0:T(8,128)(2,1)}, bf16[1,128,1024]{2,1,0:T(8,128)(2,1)}, u32[]{:S(2)}, u32[]{:S(2)}) collective-permute-start(bf16[1,128,1024]{2,1,0:T(8,128)(2,1)} %get-tuple-element.39), channel_id=1, source_target_pairs={{0,24},{8,16},{16,8},{24,0},{1,25},{9,17},{17,9},{25,1},{2,26},{10... | collective-permute-start | bytes 786440 | tf_op jit(solution)/shard_map/ppermute | solution.py:31
  490.4 49.9 %collective-permute-start.33 = (bf16[1,128,1024]{2,1,0:T(8,128)(2,1)}, bf16[1,128,1024]{2,1,0:T(8,128)(2,1)}, u32[]{:S(2)}, u32[]{:S(2)}) collective-permute-start(bf16[1,128,1024]{2,1,0:T(8,128)(2,1)} %get-tuple-element.40), channel_id=1, source_target_pairs={{0,16},{8,24},{16,0},{24,8},{1,17},{9,25},{17,1},{25,9},{2,18},{10... | collective-permute-start | bytes 786440 | tf_op jit(solution)/shard_map/ppermute | solution.py:31
  494.3 46.0 %collective-permute-start.32 = (bf16[1,128,1024]{2,1,0:T(8,128)(2,1)}, bf16[1,128,1024]{2,1,0:T(8,128)(2,1)}, u32[]{:S(2)}, u32[]{:S(2)}) collective-permute-start(bf16[1,128,1024]{2,1,0:T(8,128)(2,1)} %get-tuple-element.41), channel_id=1, source_target_pairs={{0,8},{8,0},{16,24},{24,16},{1,9},{9,1},{17,25},{25,17},{2,10},{10... | collective-permute-start | bytes 786440 | tf_op jit(solution)/shard_map/ppermute | solution.py:31
  (74 other events, 1034.6 us)
Sparse Core Ops, SparseCore 0:
  283.0 24.8 reduce-scatter.4
  368.4 67.6 reduce-scatter.6
